TPU v7x, 32 devices: a whole 2x2x4 slice. The times are simulated.
32 devices in a mesh: sub: 16 (over z, y, core), strip: 2 (over x).
Axes of the slice: x: 2, y: 2, z: 4, core: 2. Of those that a mesh axis runs over, the one named last changes fastest.
Arguments:
- spectra: bfloat16 [32, 256, 2048], P('sub', 'strip'), may hold values from -6 to 6
- offsets: int32 [32], P('sub'), may hold values from 0 to 1023
Outputs:
- foreground: float32 [1024, 256, 32], P('strip', 'sub')
All inputs are finite; a program needn't handle non-finite values.
Results may differ from a plain program's by a relative error of at most 0.0068.
Values may be sent and summed in bfloat16 or wider, within the bound.
A program may use at most 64 MiB of HBM per device.

v0:
```python
import math
import jax
import jax.numpy as jnp
import numpy as np
from jax import lax
from jax.sharding import PartitionSpec as P

KR = 256
ROWS = 1024
COLS = 256
WIN = 8
BG = 16


def from_behind(value, axis, steps):
    count = lax.axis_size(axis)
    pairs = [(source, (source + steps) % count) for source in range(count)]
    return lax.ppermute(value, axis, pairs)


def extended(shard, sides, width):
    for axis, dim in sides:
        count, length = (lax.axis_size(axis), shard.shape[dim])
        up = [(i, (i + 1) % count) for i in range(count - 1)]
        down = [(j, i) for i, j in up]
        last = lax.slice_in_dim(shard, length - width, length, axis=dim)
        leading = lax.slice_in_dim(shard, 0, width, axis=dim)
        before = lax.ppermute(last, axis, up)
        after = lax.ppermute(leading, axis, down)
        shard = jnp.concatenate([before, shard, after], axis=dim)
    return shard


def column_table(samples, width):
    sample_index = jnp.arange(samples, dtype=jnp.int32)[:, None]
    column_index = jnp.arange(width, dtype=jnp.int32)[None, :]
    phase = jnp.mod(sample_index * column_index, samples).astype(jnp.float32) * (
        2.0 * math.pi / samples
    )
    cosine = jnp.cos(phase) / math.sqrt(samples)
    sine = -jnp.sin(phase) / math.sqrt(samples)
    upper = jnp.concatenate([cosine, sine], axis=1)
    lower = jnp.concatenate([-sine, cosine], axis=1)
    return jnp.concatenate([upper, lower], axis=0).astype(jnp.bfloat16)


def row_table(row_index, samples, image_rows):
    sample_index = jnp.arange(samples, dtype=jnp.int32)[None, :] - samples // 2
    phase = jnp.mod(row_index[:, None] * sample_index, image_rows).astype(jnp.float32) * (
        2.0 * math.pi / image_rows
    )
    scale = 1.0 / math.sqrt(samples)
    return jnp.concatenate([jnp.cos(phase) * scale, jnp.sin(phase) * scale], axis=0).astype(
        jnp.bfloat16
    )


def apply_phase(mixed, offsets, sample_index):
    angle = jnp.mod(offsets[:, None] * (sample_index[None, :] - KR // 2), ROWS).astype(
        jnp.float32
    ) * (2.0 * math.pi / ROWS)
    cosine = jnp.cos(angle)[:, :, None]
    sine = jnp.sin(angle)[:, :, None]
    real_part = mixed[:, :, :COLS]
    imag_part = mixed[:, :, COLS:]
    return jnp.concatenate(
        [real_part * cosine - imag_part * sine, real_part * sine + imag_part * cosine], axis=2
    ).astype(jnp.bfloat16)


def window_mask(block_offset, count):
    target = np.arange(count)[:, None]
    source = np.arange(count)[None, :]
    distance = block_offset * count + source - target
    return ((distance >= 0) & (distance < WIN)).astype(np.float32)


def combine_parts(product, strip_rows):
    product = lax.optimization_barrier(product)
    real_part = product[:, :strip_rows, :COLS] - product[:, strip_rows:, COLS:]
    imag_part = product[:, :strip_rows, COLS:] + product[:, strip_rows:, :COLS]
    return jnp.concatenate([real_part, imag_part], axis=2)


def remove_background(stack):
    frame_count = stack.shape[0]
    series = jnp.transpose(stack, (1, 2, 0))
    source = jnp.arange(frame_count, dtype=jnp.int32)[:, None]
    target = jnp.arange(frame_count, dtype=jnp.int32)[None, :]
    behind = jnp.where(jnp.mod(target - source, frame_count) < BG, 1.0 / BG, 0.0).astype(
        jnp.float32
    )
    weights = jnp.where(source == target, 1.0, 0.0).astype(jnp.float32) - behind
    return jnp.einsum("rcg,gf->rcf", series, weights, precision=lax.Precision.HIGHEST)


def body(spectra, offsets):
    sub_dev = spectra.shape[0]
    strip_rows = ROWS // lax.axis_size("strip")
    local_samples = spectra.shape[1]
    first_row = lax.axis_index("strip") * strip_rows
    own_rows = first_row + jnp.arange(strip_rows, dtype=jnp.int32)
    own_samples = lax.axis_index("strip") * local_samples + jnp.arange(
        local_samples, dtype=jnp.int32
    )
    columns = column_table(spectra.shape[2] // 2, COLS)
    table = row_table(own_rows, KR, ROWS)
    passes = (WIN - 2 + sub_dev) // sub_dev
    shifted_local = apply_phase(
        jnp.einsum("skc,cn->skn", spectra, columns, preferred_element_type=jnp.float32),
        offsets,
        own_samples,
    )
    summed = jnp.einsum(
        "ab,bkn->akn",
        jnp.asarray(window_mask(0, sub_dev)),
        shifted_local.astype(jnp.float32),
        precision=lax.Precision.HIGHEST,
    )
    moving = shifted_local
    for block_offset in range(1, passes + 1):
        moving = from_behind(moving, "sub", -1)
        summed = summed + jnp.einsum(
            "ab,bkn->akn",
            jnp.asarray(window_mask(block_offset, sub_dev)),
            moving.astype(jnp.float32),
            precision=lax.Precision.HIGHEST,
        )
    table_wide = table.astype(jnp.float32)
    product = jnp.einsum(
        "mk,skn->smn",
        table_wide,
        lax.all_gather(summed, "strip", axis=1, tiled=True),
        precision=lax.Precision.HIGHEST,
    )
    frames = combine_parts(product, strip_rows)
    real_part = frames[:, :, :COLS]
    imag_part = frames[:, :, COLS:]
    log_power = jnp.log(1.0 + real_part * real_part + imag_part * imag_part)
    padded = extended(log_power, (("strip", 1),), 1)
    padded = jnp.pad(padded, ((0, 0), (0, 0), (1, 1)))
    total = jnp.zeros_like(log_power)
    for row_step in range(3):
        for col_step in range(3):
            total = total + padded[:, row_step : row_step + strip_rows, col_step : col_step + COLS]
    filtered = total / 9.0
    return remove_background(
        lax.all_to_all(filtered, "sub", split_axis=2, concat_axis=0, tiled=True)
    )


def solution(mesh):
    in_specs = (P("sub", "strip", None), P("sub"))
    out_specs = P("strip", "sub", None)
    return jax.shard_map(body, mesh=mesh, in_specs=in_specs, out_specs=out_specs, check_vma=False)
```

profile of v0, /device:TPU:1, one launch (start us, length us, event | category | flops | bytes accessed | tf_op | source)
XLA Modules:
  0.0 140.7 jit_solution(7064883153234936964)
XLA Ops:
  6.5 4.0 %fusion.26 = bf16[1024,256]{0,1:T(8,128)(2,1)S(1)} fusion(), kind=kLoop, calls=%fused_computation.51 | loop fusion | flops 4456448 | bytes 524288 | tf_op jit(solution)/shard_map/convert.9
  10.5 4.3 %negate_convert_fusion = (bf16[1024,256]{0,1:T(8,128)(2,1)S(1)}, bf16[1024,256]{0,1:T(8,128)(2,1)S(1)}) fusion(), kind=kLoop, calls=%fused_computation.42 | loop fusion | flops 5242880 | bytes 1048576 | tf_op jit(solution)/shard_map/convert.6
  16.6 6.6 %collective-permute-done = bf16[2,128,512]{1,2,0:T(8,128)(2,1)S(1)} collective-permute-done((bf16[2,128,512]{1,2,0:T(8,128)(2,1)S(1)}, bf16[2,128,512]{1,2,0:T(8,128)(2,1)S(1)}, u32[]{:S(2)}, u32[]{:S(2)}) %collective-permute-start) | collective-permute-done | bytes 262176 | tf_op jit(solution)/shard_map/ppermute | solution.py:18
  23.2 2.7 %collective-permute-start.1 = (bf16[2,128,512]{1,2,0:T(8,128)(2,1)S(1)}, bf16[2,128,512]{1,2,0:T(8,128)(2,1)S(1)}, u32[]{:S(2)}, u32[]{:S(2)}) collective-permute-start(bf16[2,128,512]{1,2,0:T(8,128)(2,1)S(1)} %collective-permute-done), channel_id=1, source_target_pairs={{0,30},{2,0},{4,2},{6,4},{8,6},{10,8},{12,10},{14,12},{16,14},{18,... | collective-permute-start | bytes 786440 | tf_op jit(solution)/shard_map/ppermute | solution.py:18
  26.2 2.9 %collective-permute-done.1 = bf16[2,128,512]{1,2,0:T(8,128)(2,1)S(1)} collective-permute-done((bf16[2,128,512]{1,2,0:T(8,128)(2,1)S(1)}, bf16[2,128,512]{1,2,0:T(8,128)(2,1)S(1)}, u32[]{:S(2)}, u32[]{:S(2)}) %collective-permute-start.1) | collective-permute-done | bytes 262176 | tf_op jit(solution)/shard_map/ppermute | solution.py:18
  29.0 5.4 %collective-permute-start.2 = (bf16[2,128,512]{1,2,0:T(8,128)(2,1)S(1)}, bf16[2,128,512]{1,2,0:T(8,128)(2,1)S(1)}, u32[]{:S(2)}, u32[]{:S(2)}) collective-permute-start(bf16[2,128,512]{1,2,0:T(8,128)(2,1)S(1)} %collective-permute-done.1), channel_id=1, source_target_pairs={{0,30},{2,0},{4,2},{6,4},{8,6},{10,8},{12,10},{14,12},{16,14},{18,... | collective-permute-start | bytes 786440 | tf_op jit(solution)/shard_map/ppermute | solution.py:18
  34.5 1.0 fusion.74
  37.3 5.7 %collective-permute-start.3 = (bf16[2,128,512]{1,2,0:T(8,128)(2,1)S(1)}, bf16[2,128,512]{1,2,0:T(8,128)(2,1)}, u32[]{:S(2)}, u32[]{:S(2)}) collective-permute-start(bf16[2,128,512]{1,2,0:T(8,128)(2,1)S(1)} %collective-permute-done.2), channel_id=1, source_target_pairs={{0,30},{2,0},{4,2},{6,4},{8,6},{10,8},{12,10},{14,12},{16,14},{18,... | collective-permute-start | bytes 786440 | tf_op jit(solution)/shard_map/ppermute | solution.py:18
  44.4 1.8 %fusion.53 = f32[128,512,2]{1,2,0:T(2,128)} fusion(bf16[2,128,512]{2,0,1:T(2,128)(2,1)S(1)} %copy.17), kind=kOutput, calls=%fused_computation.98 | convolution fusion | flops 3145728 | bytes 786432 | tf_op jit(solution)/shard_map/ab,bkn->akn/dot_general | solution.py:123
  46.1 1.2 copy.18
  47.4 1.1 copy.19
  48.5 1.8 %fusion.75 = f32[128,512,2]{1,2,0:T(2,128)} fusion(bf16[2,128,512]{2,0,1:T(2,128)(2,1)S(1)} %copy.19, f32[2,2,1]{1,0,2:T(2,128)S(1)} %copy-done.1), kind=kOutput, calls=%fused_computation.120 | convolution fusion | flops 3145728 | bytes 786448 | tf_op jit(solution)/shard_map/ab,bkn->akn/dot_general | solution.py:123
  50.3 2.0 %copy.20 = f32[128,512,2]{0,1,2:T(8,128)} copy(f32[128,512,2]{1,2,0:T(2,128)} %fusion.75) | data formatting | bytes 1048576 | tf_op jit(solution)/shard_map/ab,bkn->akn/dot_general | solution.py:123
  52.3 2.0 %add_bitcast_fusion = f32[2,128,512]{1,2,0:T(8,128)} fusion(f32[128,512,2]{0,1,2:T(8,128)} %copy.20, f32[128,512,2]{0,1,2:T(8,128)S(1)} %copy.18, f32[128,512,2]{0,1,2:T(8,128)S(1)} %copy.16, f32[128,512,2]{0,1,2:T(8,128)S(1)} %copy.12, f32[128,512,2]{0,1,2:T(8,128)S(1)} %copy.14), kind=kLoop, calls=%fused_computation.62 | loop fusion | flops 524288 | bytes 3145728 | tf_op jit(solution)/shard_map/add | solution.py:123
  54.3 2.5 %multiply_convert_fusion.2 = (bf16[512,256]{1,0:T(8,128)(2,1)S(1)}, bf16[512,256]{1,0:T(8,128)(2,1)S(1)}) fusion(s32[256]{0:T(256)S(1)} %iota_add_fusion.1, s32[512]{0:T(512)S(1)} %iota_add_fusion), kind=kLoop, calls=%fused_computation.61 | loop fusion | flops 2359296 | bytes 527360 | tf_op jit(solution)/shard_map/convert
  56.9 23.5 %all-gather.2.cloned.1.call-done = f32[2,256,512]{1,2,0:T(8,128)} async-done(((f32[2,128,512]{1,2,0:T(8,128)}), f32[2,256,512]{1,2,0:T(8,128)}) %all-gather.2.cloned.1.call-update) | async-done | bytes 1048592 | tf_op jit(solution)/shard_map/all_gather | solution.py:133
  80.4 3.1 %convolution_bitcast_fusion = f32[2,1024,512]{1,2,0:T(8,128)S(1)} fusion(f32[2,256,512]{1,2,0:T(8,128)} %all-gather.2.cloned.1.call-done, bf16[512,256]{1,0:T(8,128)(2,1)S(1)} %get-tuple-element.10, bf16[512,256]{1,0:T(8,128)(2,1)S(1)} %get-tuple-element.9), kind=kOutput, calls=%fused_computation | convolution fusion | flops 3222274048 | bytes 5767168 | tf_op jit(solution)/shard_map/mk,skn->smn/dot_general | solution.py:130
  84.1 2.2 %collective-permute-start.4 = (f32[2,1,256]{1,2,0:T(8,128)S(1)}, f32[2,1,256]{1,2,0:T(8,128)S(1)}, u32[]{:S(2)}, u32[]{:S(2)}) collective-permute-start(f32[2,1,256]{1,2,0:T(8,128)S(1)} %get-tuple-element.5), channel_id=1, source_target_pairs={{0,1},{2,3},{4,5},{6,7},{8,9},{10,11},{12,13},{14,15},{16,17},{18,... | collective-permute-start | bytes 6152 | tf_op jit(solution)/shard_map/ppermute | solution.py:28
  86.3 1.3 collective-permute-start.5
  87.6 3.7 %collective-permute-done.4 = f32[2,1,256]{1,2,0:T(8,128)S(1)} collective-permute-done((f32[2,1,256]{1,2,0:T(8,128)S(1)}, f32[2,1,256]{1,2,0:T(8,128)S(1)}, u32[]{:S(2)}, u32[]{:S(2)}) %collective-permute-start.4) | collective-permute-done | bytes 2080 | tf_op jit(solution)/shard_map/ppermute | solution.py:28
  91.3 3.8 %collective-permute-done.5 = f32[2,1,256]{1,2,0:T(8,128)S(1)} collective-permute-done((f32[2,1,256]{1,2,0:T(8,128)S(1)}, f32[2,1,256]{1,2,0:T(8,128)S(1)}, u32[]{:S(2)}, u32[]{:S(2)}) %collective-permute-start.5) | collective-permute-done | bytes 2080 | tf_op jit(solution)/shard_map/ppermute | solution.py:29
  95.6 1.8 %fusion.12 = f32[2,512,256]{1,2,0:T(8,128)S(1)} fusion(f32[2,514,258]{1,2,0:T(8,128)S(1)} %select_maximum_fusion, f32[2,1,256]{1,2,0:T(8,128)S(1)} %collective-permute-done.5, f32[2,512,256]{1,2,0:T(8,128)S(1)} %fusion.18, f32[2,1,256]{1,2,0:T(8,128)S(1)} %collective-permute-done.4), kind=kLoop, calls=%fused_computation.22 | loop fusion | flops 2883584 | bytes 8392704 | tf_op jit(solution)/shard_map/div | solution.py:146
  98.2 32.4 %all_to_all.18 = f32[2,512,256]{1,0,2:T(2,128)S(1)} all-to-all(f32[2,512,256]{1,0,2:T(2,128)S(1)} %copy.9), channel_id=1, replica_groups=mesh['sub'=16,'strip'=2] {'sub'}, dimensions={2} | all-to-all | bytes 2097152 | tf_op jit(solution)/shard_map/all_to_all | solution.py:148
  131.9 2.0 %fusion.21 = f32[512,16,32]{0,2,1:T(8,128)} fusion(f32[32,512,16]{1,0,2:T(8,128)S(1)} %all_to_all.16), kind=kOutput, calls=%fused_computation.39 | convolution fusion | flops 100680704 | bytes 2097152 | tf_op jit(solution)/shard_map/rcg,gf->rcf/dot_general | solution.py:94
  (33 shorter events, 8.3 us)
Async XLA Ops:
  6.5 9.1 %copy-start = (bf16[2,128,2048]{2,1,0:T(8,128)(2,1)S(1)}, bf16[2,128,2048]{2,1,0:T(8,128)(2,1)}, u32[]{:S(2)}) copy-start(bf16[2,128,2048]{2,1,0:T(8,128)(2,1)} %param.7) | copy-start | bytes 3145732
  6.5 73.8 %all-gather.2.cloned.1.call-start = ((), (), s32[]{:S(2)}) async-start(), calls=%async_computation.1 | async-start | bytes 1572864 | tf_op jit(solution)/shard_map/all_gather | solution.py:133
  15.6 18.8 %copy-start.2 = (f32[2,2,1]{1,0,2:T(2,128)S(1)}, f32[2,2,1]{1,0,2:T(2,128)}, u32[]{:S(2)}) copy-start(f32[2,2,1]{1,0,2:T(2,128)} %constant.94) | copy-start | bytes 52
  16.5 6.7 %collective-permute-start = (bf16[2,128,512]{1,2,0:T(8,128)(2,1)S(1)}, bf16[2,128,512]{1,2,0:T(8,128)(2,1)S(1)}, u32[]{:S(2)}, u32[]{:S(2)}) collective-permute-start(bf16[2,128,512]{1,2,0:T(8,128)(2,1)S(1)} %pad_maximum_fusion.2), channel_id=1, source_target_pairs={{0,30},{2,0},{4,2},{6,4},{8,6},{10,8},{12,10},{14,12},{16,14},{18,... | collective-permute-start | bytes 786440 | tf_op jit(solution)/shard_map/ppermute | solution.py:18
  23.2 5.8 %collective-permute-start.1 = (bf16[2,128,512]{1,2,0:T(8,128)(2,1)S(1)}, bf16[2,128,512]{1,2,0:T(8,128)(2,1)S(1)}, u32[]{:S(2)}, u32[]{:S(2)}) collective-permute-start(bf16[2,128,512]{1,2,0:T(8,128)(2,1)S(1)} %collective-permute-done), channel_id=1, source_target_pairs={{0,30},{2,0},{4,2},{6,4},{8,6},{10,8},{12,10},{14,12},{16,14},{18,... | collective-permute-start | bytes 786440 | tf_op jit(solution)/shard_map/ppermute | solution.py:18
  29.0 8.2 %collective-permute-start.2 = (bf16[2,128,512]{1,2,0:T(8,128)(2,1)S(1)}, bf16[2,128,512]{1,2,0:T(8,128)(2,1)S(1)}, u32[]{:S(2)}, u32[]{:S(2)}) collective-permute-start(bf16[2,128,512]{1,2,0:T(8,128)(2,1)S(1)} %collective-permute-done.1), channel_id=1, source_target_pairs={{0,30},{2,0},{4,2},{6,4},{8,6},{10,8},{12,10},{14,12},{16,14},{18,... | collective-permute-start | bytes 786440 | tf_op jit(solution)/shard_map/ppermute | solution.py:18
  37.3 10.1 %collective-permute-start.3 = (bf16[2,128,512]{1,2,0:T(8,128)(2,1)S(1)}, bf16[2,128,512]{1,2,0:T(8,128)(2,1)}, u32[]{:S(2)}, u32[]{:S(2)}) collective-permute-start(bf16[2,128,512]{1,2,0:T(8,128)(2,1)S(1)} %collective-permute-done.2), channel_id=1, source_target_pairs={{0,30},{2,0},{4,2},{6,4},{8,6},{10,8},{12,10},{14,12},{16,14},{18,... | collective-permute-start | bytes 786440 | tf_op jit(solution)/shard_map/ppermute | solution.py:18
  43.9 4.6 %copy-start.1 = (f32[2,2,1]{1,0,2:T(2,128)S(1)}, f32[2,2,1]{1,0,2:T(2,128)}, u32[]{:S(2)}) copy-start(f32[2,2,1]{1,0,2:T(2,128)} %constant.95) | copy-start | bytes 52
  84.1 7.2 %collective-permute-start.4 = (f32[2,1,256]{1,2,0:T(8,128)S(1)}, f32[2,1,256]{1,2,0:T(8,128)S(1)}, u32[]{:S(2)}, u32[]{:S(2)}) collective-permute-start(f32[2,1,256]{1,2,0:T(8,128)S(1)} %get-tuple-element.5), channel_id=1, source_target_pairs={{0,1},{2,3},{4,5},{6,7},{8,9},{10,11},{12,13},{14,15},{16,17},{18,... | collective-permute-start | bytes 6152 | tf_op jit(solution)/shard_map/ppermute | solution.py:28
  86.3 8.8 %collective-permute-start.5 = (f32[2,1,256]{1,2,0:T(8,128)S(1)}, f32[2,1,256]{1,2,0:T(8,128)S(1)}, u32[]{:S(2)}, u32[]{:S(2)}) collective-permute-start(f32[2,1,256]{1,2,0:T(8,128)S(1)} %get-tuple-element.6), channel_id=1, source_target_pairs={{1,0},{3,2},{5,4},{7,6},{9,8},{11,10},{13,12},{15,14},{17,16},{19,... | collective-permute-start | bytes 6152 | tf_op jit(solution)/shard_map/ppermute | solution.py:29
Sparse Core Ops, SparseCore 0:
  54.4 25.8 all-gather.1
where the time goes:
time: 141 us
  waiting for transfers between devices  40.6 us (29%)
  blocking collectives  32.4 us (23%)
  starting transfers between devices  17.3 us (12%)
  other arithmetic  16.4 us (12%)
  between operations  13.7 us (10%)
  matrix products  12.3 us (9%)
  local copies, waits for them, and re-layouts  8.09 us (6%)
    all_to_all x1, blocking collectives, body(): lax.all_to_all(filtered, 'sub', split_axis=2, concat_axis=0, tiled=True)  32.4 us
    all_gather x1, waiting for transfers between devices, body(): lax.all_gather(summed, 'strip', axis=1, tiled=True)  23.5 us
    ppermute x4, starting transfers between devices, from_behind(): return lax.ppermute(value, axis, pairs)  13.9 us
    another operation x4, other arithmetic  10.9 us
    ppermute x4, waiting for transfers between devices, from_behind(): return lax.ppermute(value, axis, pairs)  9.54 us
    dot_general x4, matrix products, body(): jnp.einsum('ab,bkn->akn', jnp.asarray(window_mask(block_offset, sub_dev))...  5.45 us
    ppermute x1, waiting for transfers between devices, extended(): after = lax.ppermute(leading, axis, down)  3.85 us
    dot_general x4, local copies, waits for them, and re-layouts, body(): jnp.einsum('ab,bkn->akn', jnp.asarray(window_mask(block_offset, sub_dev))...  3.73 us
  transfers between devices with their start and end apart: 7, of which 5 were waited for; matrix products, arithmetic and copies ran while one was open for 7% of the time, Pallas kernels for 0%

commit v1 on v0

--- a/solution.py
+++ b/solution.py
@@ -144,9 +144,19 @@
         for col_step in range(3):
             total = total + padded[:, row_step : row_step + strip_rows, col_step : col_step + COLS]
     filtered = total / 9.0
-    return remove_background(
-        lax.all_to_all(filtered, "sub", split_axis=2, concat_axis=0, tiled=True)
-    )
+
+    def cycles_attach(xin):
+        local_out = lax.psum(1, axis_name="sub")
+        piece_now = lax.all_to_all(
+            jnp.stack(jnp.split(xin, local_out, axis=2), 0),
+            axis_name="sub",
+            split_axis=0,
+            concat_axis=0,
+        )
+        n_now = jnp.concatenate(piece_now, axis=0)
+        return n_now
+
+    return remove_background(cycles_attach(filtered))
 
 
 def solution(mesh):

time: 141 us -> 140 us (level)
  local copies, waits for them, and re-layouts: 8.09 us -> 6.13 us
where the time goes in v1:
time: 140 us
  waiting for transfers between devices  40.6 us (29%)
  blocking collectives  32.4 us (23%)
  starting transfers between devices  17.3 us (12%)
  other arithmetic  16.4 us (12%)
  between operations  13.8 us (10%)
  matrix products  12.9 us (9%)
  local copies, waits for them, and re-layouts  6.13 us (4%)
    all_to_all x1, blocking collectives, cycles_attach(): lax.all_to_all(jnp.stack(jnp.split(xin, local_out, axis=2), 0), axis_name...  32.4 us
    all_gather x1, waiting for transfers between devices, body(): lax.all_gather(summed, 'strip', axis=1, tiled=True)  23.5 us
    ppermute x4, starting transfers between devices, from_behind(): return lax.ppermute(value, axis, pairs)  13.9 us
    another operation x4, other arithmetic  10.9 us
    ppermute x4, waiting for transfers between devices, from_behind(): return lax.ppermute(value, axis, pairs)  9.54 us
    dot_general x4, matrix products, body(): jnp.einsum('ab,bkn->akn', jnp.asarray(window_mask(block_offset, sub_dev))...  5.45 us
    ppermute x1, waiting for transfers between devices, extended(): after = lax.ppermute(leading, axis, down)  3.85 us
    dot_general x4, local copies, waits for them, and re-layouts, body(): jnp.einsum('ab,bkn->akn', jnp.asarray(window_mask(block_offset, sub_dev))...  3.73 us
  transfers between devices with their start and end apart: 7, of which 5 were waited for; matrix products, arithmetic and copies ran while one was open for 7% of the time, Pallas kernels for 0%

profile of v1, /device:TPU:1, one launch (start us, length us, event | category | flops | bytes accessed | tf_op | source)
XLA Modules:
  0.0 139.5 jit_solution(18002861768679792401)
XLA Ops:
  6.5 4.0 %fusion.27 = bf16[1024,256]{0,1:T(8,128)(2,1)S(1)} fusion(), kind=kLoop, calls=%fused_computation.51 | loop fusion | flops 4456448 | bytes 524288 | tf_op jit(solution)/shard_map/convert.9
  10.5 4.3 %negate_convert_fusion = (bf16[1024,256]{0,1:T(8,128)(2,1)S(1)}, bf16[1024,256]{0,1:T(8,128)(2,1)S(1)}) fusion(), kind=kLoop, calls=%fused_computation.42 | loop fusion | flops 5242880 | bytes 1048576 | tf_op jit(solution)/shard_map/convert.6
  16.6 6.6 %collective-permute-done = bf16[2,128,512]{1,2,0:T(8,128)(2,1)S(1)} collective-permute-done((bf16[2,128,512]{1,2,0:T(8,128)(2,1)S(1)}, bf16[2,128,512]{1,2,0:T(8,128)(2,1)S(1)}, u32[]{:S(2)}, u32[]{:S(2)}) %collective-permute-start) | collective-permute-done | bytes 262176 | tf_op jit(solution)/shard_map/ppermute | solution.py:18
  23.2 2.7 %collective-permute-start.1 = (bf16[2,128,512]{1,2,0:T(8,128)(2,1)S(1)}, bf16[2,128,512]{1,2,0:T(8,128)(2,1)S(1)}, u32[]{:S(2)}, u32[]{:S(2)}) collective-permute-start(bf16[2,128,512]{1,2,0:T(8,128)(2,1)S(1)} %collective-permute-done), channel_id=1, source_target_pairs={{0,30},{2,0},{4,2},{6,4},{8,6},{10,8},{12,10},{14,12},{16,14},{18,... | collective-permute-start | bytes 786440 | tf_op jit(solution)/shard_map/ppermute | solution.py:18
  26.2 2.9 %collective-permute-done.1 = bf16[2,128,512]{1,2,0:T(8,128)(2,1)S(1)} collective-permute-done((bf16[2,128,512]{1,2,0:T(8,128)(2,1)S(1)}, bf16[2,128,512]{1,2,0:T(8,128)(2,1)S(1)}, u32[]{:S(2)}, u32[]{:S(2)}) %collective-permute-start.1) | collective-permute-done | bytes 262176 | tf_op jit(solution)/shard_map/ppermute | solution.py:18
  29.0 5.4 %collective-permute-start.2 = (bf16[2,128,512]{1,2,0:T(8,128)(2,1)S(1)}, bf16[2,128,512]{1,2,0:T(8,128)(2,1)S(1)}, u32[]{:S(2)}, u32[]{:S(2)}) collective-permute-start(bf16[2,128,512]{1,2,0:T(8,128)(2,1)S(1)} %collective-permute-done.1), channel_id=1, source_target_pairs={{0,30},{2,0},{4,2},{6,4},{8,6},{10,8},{12,10},{14,12},{16,14},{18,... | collective-permute-start | bytes 786440 | tf_op jit(solution)/shard_map/ppermute | solution.py:18
  34.5 1.0 fusion.91
  37.3 5.7 %collective-permute-start.3 = (bf16[2,128,512]{1,2,0:T(8,128)(2,1)S(1)}, bf16[2,128,512]{1,2,0:T(8,128)(2,1)}, u32[]{:S(2)}, u32[]{:S(2)}) collective-permute-start(bf16[2,128,512]{1,2,0:T(8,128)(2,1)S(1)} %collective-permute-done.2), channel_id=1, source_target_pairs={{0,30},{2,0},{4,2},{6,4},{8,6},{10,8},{12,10},{14,12},{16,14},{18,... | collective-permute-start | bytes 786440 | tf_op jit(solution)/shard_map/ppermute | solution.py:18
  44.4 1.8 %fusion.70 = f32[128,512,2]{1,2,0:T(2,128)} fusion(bf16[2,128,512]{2,0,1:T(2,128)(2,1)S(1)} %copy.15), kind=kOutput, calls=%fused_computation.130 | convolution fusion | flops 3145728 | bytes 786432 | tf_op jit(solution)/shard_map/ab,bkn->akn/dot_general | solution.py:123
  46.1 1.2 copy.16
  47.4 1.1 copy.17
  48.5 1.8 %fusion.92 = f32[128,512,2]{1,2,0:T(2,128)} fusion(bf16[2,128,512]{2,0,1:T(2,128)(2,1)S(1)} %copy.17, f32[2,2,1]{1,0,2:T(2,128)S(1)} %copy-done.1), kind=kOutput, calls=%fused_computation.152 | convolution fusion | flops 3145728 | bytes 786448 | tf_op jit(solution)/shard_map/ab,bkn->akn/dot_general | solution.py:123
  50.3 2.0 %copy.18 = f32[128,512,2]{0,1,2:T(8,128)} copy(f32[128,512,2]{1,2,0:T(2,128)} %fusion.92) | data formatting | bytes 1048576 | tf_op jit(solution)/shard_map/ab,bkn->akn/dot_general | solution.py:123
  52.3 2.0 %add_bitcast_fusion = f32[2,128,512]{1,2,0:T(8,128)} fusion(f32[128,512,2]{0,1,2:T(8,128)} %copy.18, f32[128,512,2]{0,1,2:T(8,128)S(1)} %copy.16, f32[128,512,2]{0,1,2:T(8,128)S(1)} %copy.14, f32[128,512,2]{0,1,2:T(8,128)S(1)} %copy.10, f32[128,512,2]{0,1,2:T(8,128)S(1)} %copy.12), kind=kLoop, calls=%fused_computation.62 | loop fusion | flops 524288 | bytes 3145728 | tf_op jit(solution)/shard_map/add | solution.py:123
  54.3 2.5 %multiply_convert_fusion.2 = (bf16[512,256]{1,0:T(8,128)(2,1)S(1)}, bf16[512,256]{1,0:T(8,128)(2,1)S(1)}) fusion(s32[256]{0:T(256)S(1)} %iota_add_fusion.1, s32[512]{0:T(512)S(1)} %iota_add_fusion), kind=kLoop, calls=%fused_computation.61 | loop fusion | flops 2359296 | bytes 527360 | tf_op jit(solution)/shard_map/convert
  56.9 23.5 %all-gather.2.cloned.1.call-done = f32[2,256,512]{1,2,0:T(8,128)} async-done(((f32[2,128,512]{1,2,0:T(8,128)}), f32[2,256,512]{1,2,0:T(8,128)}) %all-gather.2.cloned.1.call-update) | async-done | bytes 1048592 | tf_op jit(solution)/shard_map/all_gather | solution.py:133
  80.4 3.1 %convolution_bitcast_fusion = f32[2,1024,512]{1,2,0:T(8,128)S(1)} fusion(f32[2,256,512]{1,2,0:T(8,128)} %all-gather.2.cloned.1.call-done, bf16[512,256]{1,0:T(8,128)(2,1)S(1)} %get-tuple-element.10, bf16[512,256]{1,0:T(8,128)(2,1)S(1)} %get-tuple-element.9), kind=kOutput, calls=%fused_computation | convolution fusion | flops 3222274048 | bytes 5767168 | tf_op jit(solution)/shard_map/mk,skn->smn/dot_general | solution.py:130
  84.1 2.2 %collective-permute-start.4 = (f32[2,1,256]{1,2,0:T(8,128)S(1)}, f32[2,1,256]{1,2,0:T(8,128)S(1)}, u32[]{:S(2)}, u32[]{:S(2)}) collective-permute-start(f32[2,1,256]{1,2,0:T(8,128)S(1)} %get-tuple-element.5), channel_id=1, source_target_pairs={{0,1},{2,3},{4,5},{6,7},{8,9},{10,11},{12,13},{14,15},{16,17},{18,... | collective-permute-start | bytes 6152 | tf_op jit(solution)/shard_map/ppermute | solution.py:28
  86.3 1.3 collective-permute-start.5
  87.6 3.7 %collective-permute-done.4 = f32[2,1,256]{1,2,0:T(8,128)S(1)} collective-permute-done((f32[2,1,256]{1,2,0:T(8,128)S(1)}, f32[2,1,256]{1,2,0:T(8,128)S(1)}, u32[]{:S(2)}, u32[]{:S(2)}) %collective-permute-start.4) | collective-permute-done | bytes 2080 | tf_op jit(solution)/shard_map/ppermute | solution.py:28
  91.3 3.8 %collective-permute-done.5 = f32[2,1,256]{1,2,0:T(8,128)S(1)} collective-permute-done((f32[2,1,256]{1,2,0:T(8,128)S(1)}, f32[2,1,256]{1,2,0:T(8,128)S(1)}, u32[]{:S(2)}, u32[]{:S(2)}) %collective-permute-start.5) | collective-permute-done | bytes 2080 | tf_op jit(solution)/shard_map/ppermute | solution.py:29
  95.6 1.8 %fusion.12 = f32[2,512,256]{1,2,0:T(8,128)S(1)} fusion(f32[2,514,258]{1,2,0:T(8,128)S(1)} %select_maximum_fusion, f32[2,1,256]{1,2,0:T(8,128)S(1)} %collective-permute-done.5, f32[2,512,256]{1,2,0:T(8,128)S(1)} %fusion.18, f32[2,1,256]{1,2,0:T(8,128)S(1)} %collective-permute-done.4), kind=kLoop, calls=%fused_computation.22 | loop fusion | flops 2883584 | bytes 8392704 | tf_op jit(solution)/shard_map/div | solution.py:146
  97.7 32.4 %all_to_all.5 = f32[16,2,512,16]{2,3,1,0:T(8,128)S(1)} all-to-all(f32[16,2,512,16]{2,3,1,0:T(8,128)S(1)} %fusion.33), channel_id=1, replica_groups=mesh['sub'=16,'strip'=2] {'sub'}, dimensions={0} | all-to-all | bytes 2097152 | tf_op jit(solution)/shard_map/all_to_all | solution.py:150
  130.0 2.7 %fusion.21 = f32[512,16,32]{0,2,1:T(8,128)} fusion(f32[32,512,16]{1,2,0:T(8,128)S(1)} %bitcast.96), kind=kOutput, calls=%fused_computation.39 | convolution fusion | flops 100680704 | bytes 2097152 | tf_op jit(solution)/shard_map/rcg,gf->rcf/dot_general | solution.py:94
  (46 shorter events, 6.4 us)
Async XLA Ops:
  6.5 9.1 %copy-start = (bf16[2,128,2048]{2,1,0:T(8,128)(2,1)S(1)}, bf16[2,128,2048]{2,1,0:T(8,128)(2,1)}, u32[]{:S(2)}) copy-start(bf16[2,128,2048]{2,1,0:T(8,128)(2,1)} %param.7) | copy-start | bytes 3145732
  6.5 73.8 %all-gather.2.cloned.1.call-start = ((), (), s32[]{:S(2)}) async-start(), calls=%async_computation.1 | async-start | bytes 1572864 | tf_op jit(solution)/shard_map/all_gather | solution.py:133
  15.6 18.8 %copy-start.2 = (f32[2,2,1]{1,0,2:T(2,128)S(1)}, f32[2,2,1]{1,0,2:T(2,128)}, u32[]{:S(2)}) copy-start(f32[2,2,1]{1,0,2:T(2,128)} %constant.94) | copy-start | bytes 52
  16.5 6.7 %collective-permute-start = (bf16[2,128,512]{1,2,0:T(8,128)(2,1)S(1)}, bf16[2,128,512]{1,2,0:T(8,128)(2,1)S(1)}, u32[]{:S(2)}, u32[]{:S(2)}) collective-permute-start(bf16[2,128,512]{1,2,0:T(8,128)(2,1)S(1)} %pad_maximum_fusion.2), channel_id=1, source_target_pairs={{0,30},{2,0},{4,2},{6,4},{8,6},{10,8},{12,10},{14,12},{16,14},{18,... | collective-permute-start | bytes 786440 | tf_op jit(solution)/shard_map/ppermute | solution.py:18
  23.2 5.8 %collective-permute-start.1 = (bf16[2,128,512]{1,2,0:T(8,128)(2,1)S(1)}, bf16[2,128,512]{1,2,0:T(8,128)(2,1)S(1)}, u32[]{:S(2)}, u32[]{:S(2)}) collective-permute-start(bf16[2,128,512]{1,2,0:T(8,128)(2,1)S(1)} %collective-permute-done), channel_id=1, source_target_pairs={{0,30},{2,0},{4,2},{6,4},{8,6},{10,8},{12,10},{14,12},{16,14},{18,... | collective-permute-start | bytes 786440 | tf_op jit(solution)/shard_map/ppermute | solution.py:18
  29.0 8.2 %collective-permute-start.2 = (bf16[2,128,512]{1,2,0:T(8,128)(2,1)S(1)}, bf16[2,128,512]{1,2,0:T(8,128)(2,1)S(1)}, u32[]{:S(2)}, u32[]{:S(2)}) collective-permute-start(bf16[2,128,512]{1,2,0:T(8,128)(2,1)S(1)} %collective-permute-done.1), channel_id=1, source_target_pairs={{0,30},{2,0},{4,2},{6,4},{8,6},{10,8},{12,10},{14,12},{16,14},{18,... | collective-permute-start | bytes 786440 | tf_op jit(solution)/shard_map/ppermute | solution.py:18
  37.3 10.1 %collective-permute-start.3 = (bf16[2,128,512]{1,2,0:T(8,128)(2,1)S(1)}, bf16[2,128,512]{1,2,0:T(8,128)(2,1)}, u32[]{:S(2)}, u32[]{:S(2)}) collective-permute-start(bf16[2,128,512]{1,2,0:T(8,128)(2,1)S(1)} %collective-permute-done.2), channel_id=1, source_target_pairs={{0,30},{2,0},{4,2},{6,4},{8,6},{10,8},{12,10},{14,12},{16,14},{18,... | collective-permute-start | bytes 786440 | tf_op jit(solution)/shard_map/ppermute | solution.py:18
  43.9 4.6 %copy-start.1 = (f32[2,2,1]{1,0,2:T(2,128)S(1)}, f32[2,2,1]{1,0,2:T(2,128)}, u32[]{:S(2)}) copy-start(f32[2,2,1]{1,0,2:T(2,128)} %constant.95) | copy-start | bytes 52
  84.1 7.2 %collective-permute-start.4 = (f32[2,1,256]{1,2,0:T(8,128)S(1)}, f32[2,1,256]{1,2,0:T(8,128)S(1)}, u32[]{:S(2)}, u32[]{:S(2)}) collective-permute-start(f32[2,1,256]{1,2,0:T(8,128)S(1)} %get-tuple-element.5), channel_id=1, source_target_pairs={{0,1},{2,3},{4,5},{6,7},{8,9},{10,11},{12,13},{14,15},{16,17},{18,... | collective-permute-start | bytes 6152 | tf_op jit(solution)/shard_map/ppermute | solution.py:28
  86.3 8.8 %collective-permute-start.5 = (f32[2,1,256]{1,2,0:T(8,128)S(1)}, f32[2,1,256]{1,2,0:T(8,128)S(1)}, u32[]{:S(2)}, u32[]{:S(2)}) collective-permute-start(f32[2,1,256]{1,2,0:T(8,128)S(1)} %get-tuple-element.6), channel_id=1, source_target_pairs={{1,0},{3,2},{5,4},{7,6},{9,8},{11,10},{13,12},{15,14},{17,16},{19,... | collective-permute-start | bytes 6152 | tf_op jit(solution)/shard_map/ppermute | solution.py:29
Sparse Core Ops, SparseCore 0:
  54.4 25.8 all-gather.1
